TPU v7x, 32 devices: a whole 2x2x4 slice. The times are simulated.
32 devices in a mesh: span: 8 (over z, x), chord: 4 (over y, core).
Axes of the slice: x: 2, y: 2, z: 4, core: 2. Of those that a mesh axis runs over, the one named last changes fastest.
Arguments:
- pressure: float32 [2, 1024, 512], P(None, 'span', 'chord'), may hold values from 0 to 1
- fill_state: int32 [2, 1024, 512], P(None, 'span', 'chord'), may hold values from 0 to 2
- perm_class: int32 [2, 1024, 512], P(None, 'span', 'chord'), may hold values from 0 to 7
- perm_table: float32 [2, 8], replicated, may hold values from 1 to 4
- inlet_span: int32 [128], replicated, may hold values from 0 to 1023
- inlet_chord: int32 [128], replicated, may hold values from 0 to 511
- inlet_rate: float32 [128], replicated, may hold values from 500 to 1500
Outputs:
- pressure_out: float32 [2, 1024, 512], P(None, 'span', 'chord')
Inputs may be any that keep to these rules, and one draw needn't show every extreme that they name: `inlet_span`: inlet cells may repeat; their rates add.
All inputs are finite; a program needn't handle non-finite values.
Results may differ from a plain program's by a relative error of at most 0.00035.
Values sent between devices are 32-bit elements; how exact they have to be, the bound alone decides.
A program may use at most 64 MiB of HBM per device.

v0:
```python
import jax
import jax.numpy as jnp
from jax import lax
from jax.sharding import PartitionSpec as P

HALF_RATE = 200.0
COUPLE = 0.3


def shift_lower(values, stride):
    padding = jnp.zeros(values.shape[:-1] + (stride,), values.dtype)
    return jnp.concatenate([padding, values[..., :-stride]], axis=-1)


def shift_upper(values, stride):
    padding = jnp.zeros(values.shape[:-1] + (stride,), values.dtype)
    return jnp.concatenate([values[..., stride:], padding], axis=-1)


def faces(cond):
    summed = HALF_RATE * (cond + shift_upper(cond, 1))
    closing = jnp.zeros(cond.shape[:-1] + (1,), cond.dtype)
    return jnp.concatenate([summed[..., :-1], closing], axis=-1)


def parallel_cyclic_reduction_update(
    lower_band,
    diagonal_terms,
    upper_band,
    right_hand_side,
    previous_neighbour_row,
    next_neighbour_row,
):
    new_lower = -lower_band * previous_neighbour_row[0]
    new_diag = (
        diagonal_terms - lower_band * previous_neighbour_row[1] - upper_band * next_neighbour_row[0]
    )
    new_upper = -upper_band * next_neighbour_row[1]
    new_rhs = (
        right_hand_side
        - lower_band * previous_neighbour_row[2]
        - upper_band * next_neighbour_row[2]
    )
    return (new_lower, new_diag, new_upper, new_rhs)


def line_solve(lower_band, diagonal_terms, upper_band, right_hand_side):
    total = right_hand_side.shape[-1]
    stride = 1
    while stride < total:
        ratios = (
            lower_band / diagonal_terms,
            upper_band / diagonal_terms,
            right_hand_side / diagonal_terms,
        )
        previous_neighbour_row = [shift_lower(v, stride) for v in ratios]
        next_neighbour_row = [shift_upper(v, stride) for v in ratios]
        lower_band, diagonal_terms, upper_band, right_hand_side = parallel_cyclic_reduction_update(
            lower_band,
            diagonal_terms,
            upper_band,
            right_hand_side,
            previous_neighbour_row,
            next_neighbour_row,
        )
        stride = stride * 2
    return right_hand_side / diagonal_terms


def explicit_core(field, field_next, field_prev, faces_here, faces_prev, source):
    flux = faces_here * (field_next - field) - faces_prev * (field - field_prev)
    return field + flux + COUPLE * (jnp.flip(field, 0) - field) + source


def explicit_lines(field, faces_here, faces_prev, source):
    return explicit_core(
        field, shift_upper(field, 1), shift_lower(field, 1), faces_here, faces_prev, source
    )


def second_half(star, half_lines, source):
    return 2.0 * star - half_lines + COUPLE * (jnp.flip(star, 0) - star) + source


def to_span(block):
    turned = jnp.transpose(block, (0, 2, 1))
    return lax.all_to_all(turned, "span", split_axis=1, concat_axis=2, tiled=True)


def span_return(lines):
    turned = lax.all_to_all(lines, "span", split_axis=2, concat_axis=1, tiled=True)
    return jnp.transpose(turned, (0, 2, 1))


def to_chord(block):
    return lax.all_to_all(block, "chord", split_axis=1, concat_axis=2, tiled=True)


def from_chord(lines):
    return lax.all_to_all(lines, "chord", split_axis=2, concat_axis=1, tiled=True)


def per_device(pressure, fill_state, perm_class, perm_table, inlet_span, inlet_chord, inlet_rate):
    plies = pressure.shape[0]
    rows = pressure.shape[1]
    width = pressure.shape[2]
    mobility = jnp.where(fill_state == 0, 1.0, jnp.where(fill_state == 1, 0.5, 0.25))
    perm = jnp.zeros(pressure.shape, jnp.float32)
    for klass in range(perm_table.shape[1]):
        perm = perm + jnp.where(perm_class == klass, perm_table[:, klass][:, None, None], 0.0)
    cond = perm * mobility
    row_global = lax.axis_index("span") * rows + jnp.arange(rows, dtype=jnp.int32)
    col_global = lax.axis_index("chord") * width + jnp.arange(width, dtype=jnp.int32)
    row_hits = (row_global[:, None] == inlet_span[None, :]).astype(jnp.float32) * inlet_rate[
        None, :
    ]
    col_hits = (inlet_chord[:, None] == col_global[None, :]).astype(jnp.float32)
    plane = jnp.dot(
        row_hits, col_hits, precision=lax.Precision.HIGHEST, preferred_element_type=jnp.float32
    )
    source = plane[None]
    span_setup = to_span(jnp.concatenate([cond, source], axis=0))
    span_faces = faces(span_setup[:plies])
    span_prev = shift_lower(span_faces, 1)
    span_source = span_setup[plies:]
    span_diag = 1.0 + span_prev + span_faces
    chord_setup = to_chord(jnp.concatenate([cond, source, pressure], axis=0))
    chord_faces = faces(chord_setup[:plies])
    chord_prev = shift_lower(chord_faces, 1)
    chord_diag = 1.0 + chord_prev + chord_faces
    chord_source = chord_setup[plies : plies + 1]
    field = chord_setup[plies + 1 :]
    half = explicit_lines(field, chord_faces, chord_prev, chord_source)
    half_lines = to_span(from_chord(half))
    star = line_solve(-span_prev, span_diag, -span_faces, half_lines)
    second = second_half(star, half_lines, span_source)
    returned = to_chord(span_return(second))
    field = line_solve(-chord_prev, chord_diag, -chord_faces, returned)
    result = from_chord(field)
    return result


def solution(mesh):
    placed = (
        P(None, "span", "chord"),
        P(None, "span", "chord"),
        P(None, "span", "chord"),
        P(),
        P(),
        P(),
        P(),
    )
    return jax.shard_map(
        per_device, mesh=mesh, in_specs=placed, out_specs=P(None, "span", "chord"), check_vma=False
    )
```

profile of v0, /device:TPU:0, one launch (start us, length us, event | category | flops | bytes accessed | tf_op | source)
XLA Modules:
  0.0 96.3 jit_solution(14580648930356081755)
XLA Ops:
  0.0 0.7 copy-done.2
  0.7 0.3 slice_reduce_fusion.7
  1.0 1.0 %copy.86 = f32[2,128,128]{2,0,1:T(2,128)S(1)} copy(f32[2,128,128]{2,1,0:T(8,128)} %param.7) | data formatting | bytes 262144 | tf_op args[0]
  2.1 0.2 fusion.16
  2.4 0.6 copy-done
  3.0 0.6 fusion.13
  3.5 1.0 %pad_maximum_fusion = f32[5,128,128]{2,0,1:T(8,128)} fusion(f32[2,128,128]{2,0,1:T(2,128)S(1)} %copy.86, f32[1,128,128]{2,0,1:T(1,128)S(1)} %bitcast.122, f32[2,128,128]{2,0,1:T(2,128)S(1)} %fusion.13), kind=kLoop, calls=%fused_computation | loop fusion | flops 163840 | bytes 655360 | tf_op jit(solution)/shard_map/concatenate | solution.py:127
  4.5 4.3 %all-to-all-start = ((f32[5,128,128]{2,0,1:T(8,128)}), f32[5,128,128]{2,0,1:T(8,128)S(1)}, u32[]{:S(2)}, u32[]{:S(2)}) async-start(f32[5,128,128]{2,0,1:T(8,128)} %pad_maximum_fusion), calls=%async_computation | async-start | bytes 1048576 | tf_op jit(solution)/shard_map/all_to_all | solution.py:96
  8.8 0.1 maximum_bitcast_fusion
  8.9 0.9 copy.98
  9.8 7.8 %all-to-all-done = f32[5,128,128]{2,0,1:T(8,128)S(1)} async-done(((f32[5,128,128]{2,0,1:T(8,128)}), f32[5,128,128]{2,0,1:T(8,128)S(1)}, u32[]{:S(2)}, u32[]{:S(2)}) %all-to-all-start) | async-done | bytes 327712 | tf_op jit(solution)/shard_map/all_to_all | solution.py:96
  17.6 6.5 %all-to-all-start.3 = ((f32[3,128,128]{2,0,1:T(4,128)}), f32[3,128,128]{2,0,1:T(4,128)S(1)}, u32[]{:S(2)}, u32[]{:S(2)}) async-start(f32[3,128,128]{2,0,1:T(4,128)} %copy.98), calls=%async_computation.3 | async-start | bytes 524288 | tf_op jit(solution)/shard_map/all_to_all | solution.py:87
  24.5 0.6 copy-done.4
  25.2 0.1 fusion.2
  25.3 0.2 copy.91
  25.6 1.2 %reshape.34 = f32[4,1,8192]{2,1,0:T(1,128)} reshape(f32[512,2,32]{2,1,0:T(2,128)S(1)} %bitcast.97) | data formatting | bytes 262144
  26.8 5.9 %all-to-all-done.3 = f32[3,128,128]{2,0,1:T(4,128)S(1)} async-done(((f32[3,128,128]{2,0,1:T(4,128)}), f32[3,128,128]{2,0,1:T(4,128)S(1)}, u32[]{:S(2)}, u32[]{:S(2)}) %all-to-all-start.3) | async-done | bytes 196640 | tf_op jit(solution)/shard_map/all_to_all | solution.py:87
  32.7 3.3 %all-to-all-start.1 = ((f32[4,1,8192]{2,1,0:T(1,128)}), f32[4,1,8192]{2,1,0:T(1,128)S(1)}, u32[]{:S(2)}, u32[]{:S(2)}) async-start(f32[4,1,8192]{2,1,0:T(1,128)} %reshape.34), calls=%async_computation.1 | async-start | bytes 262144 | tf_op jit(solution)/shard_map/all_to_all | solution.py:100
  36.2 4.4 %all-to-all-done.1 = f32[4,1,8192]{2,1,0:T(1,128)S(1)} async-done(((f32[4,1,8192]{2,1,0:T(1,128)}), f32[4,1,8192]{2,1,0:T(1,128)S(1)}, u32[]{:S(2)}, u32[]{:S(2)}) %all-to-all-start.1) | async-done | bytes 131104 | tf_op jit(solution)/shard_map/all_to_all | solution.py:100
  40.6 0.6 broadcast.342
  41.2 1.0 %reduce.16 = f32[4,8192]{1,0:T(4,128)S(1)} reduce(f32[4,1,8192]{2,1,0:T(1,128)S(1)} %all-to-all-done.1, f32[]{:T(128)} %broadcast.342), dimensions={1}, to_apply=%all_to_all.90.reduce_sub_computation | reduce | bytes 262148 | tf_op jit(solution)/shard_map/all_to_all | solution.py:100
  42.2 0.5 reshape.35
  42.7 0.2 copy.111
  42.9 0.8 copy.94
  43.6 3.6 %all-to-all-start.2 = ((f32[2,128,128]{2,0,1:T(2,128)}), f32[2,128,128]{2,0,1:T(2,128)S(1)}, u32[]{:S(2)}, u32[]{:S(2)}) async-start(f32[2,128,128]{2,0,1:T(2,128)} %copy.94), calls=%async_computation.2 | async-start | bytes 262144 | tf_op jit(solution)/shard_map/all_to_all | solution.py:87
  47.2 7.3 %all-to-all-done.2 = f32[2,128,128]{2,0,1:T(2,128)S(1)} async-done(((f32[2,128,128]{2,0,1:T(2,128)}), f32[2,128,128]{2,0,1:T(2,128)S(1)}, u32[]{:S(2)}, u32[]{:S(2)}) %all-to-all-start.2) | async-done | bytes 131104 | tf_op jit(solution)/shard_map/all_to_all | solution.py:87
  54.6 0.7 copy-done.3
  55.3 0.1 negate_divide_fusion.2
  55.7 0.2 fusion.44
  55.9 0.1 fusion.60
  56.3 0.1 fusion.43
  56.9 0.1 fusion.42
  57.5 0.1 fusion.41
  58.0 0.1 fusion.40
  58.6 0.1 fusion.39
  59.2 0.1 fusion.38
  60.0 0.5 copy.102
  60.5 1.4 %reshape.36 = f32[8,1,4096]{2,1,0:T(1,128)S(1)} reshape(f32[1024,2,16]{2,1,0:T(2,128)S(1)} %bitcast.95) | data formatting | bytes 262144
  62.0 9.7 %all_to_all.120 = f32[8,1,4096]{2,1,0:T(1,128)S(1)} all-to-all(f32[8,1,4096]{2,1,0:T(1,128)S(1)} %reshape.36), channel_id=1, replica_groups=mesh['span'=8,'chord'=4] {'span'}, dimensions={0} | all-to-all | bytes 262144 | tf_op jit(solution)/shard_map/all_to_all | solution.py:91
  71.7 1.0 %reduce.17 = f32[8,4096]{1,0:T(8,128)S(1)} reduce(f32[8,1,4096]{2,1,0:T(1,128)S(1)} %all_to_all.120, f32[]{:T(128)} %broadcast.342), dimensions={1}, to_apply=%all_to_all.101.reduce_sub_computation | reduce | bytes 262148 | tf_op jit(solution)/shard_map/all_to_all | solution.py:91
  72.7 1.4 %reshape.37 = f32[1024,2,16]{2,1,0:T(2,128)S(1)} reshape(f32[8,4096]{1,0:T(8,128)S(1)} %reduce.17) | data formatting | bytes 262144
  74.1 0.4 copy.113
  74.5 0.1 copy.105
  74.6 7.0 %all_to_all.121 = f32[2,128,128]{2,0,1:T(2,128)S(1)} all-to-all(f32[2,128,128]{2,0,1:T(2,128)S(1)} %copy.105), channel_id=1, replica_groups=mesh['span'=8,'chord'=4] {'chord'}, dimensions={1} | all-to-all | bytes 262144 | tf_op jit(solution)/shard_map/all_to_all | solution.py:96
  81.6 0.1 negate_divide_fusion
  82.1 0.2 fusion.34
  82.3 0.1 fusion.74
  82.7 0.1 fusion.33
  82.9 0.1 fusion.72
  83.3 0.1 fusion.32
  83.5 0.1 fusion.70
  83.9 0.1 fusion.31
  84.0 0.1 fusion.68
  84.5 0.1 fusion.30
  85.0 0.1 fusion.29
  85.6 0.1 fusion.28
  85.8 0.1 fusion.62
  86.2 0.2 copy.108
  86.4 0.5 reshape.38
  87.0 7.0 %all_to_all.122 = f32[4,1,8192]{2,1,0:T(1,128)S(1)} all-to-all(f32[4,1,8192]{2,1,0:T(1,128)S(1)} %reshape.38), channel_id=1, replica_groups=mesh['span'=8,'chord'=4] {'chord'}, dimensions={0} | all-to-all | bytes 262144 | tf_op jit(solution)/shard_map/all_to_all | solution.py:100
  94.0 1.0 %reduce.18 = f32[4,8192]{1,0:T(4,128)S(1)} reduce(f32[4,1,8192]{2,1,0:T(1,128)S(1)} %all_to_all.122, f32[]{:T(128)} %broadcast.342), dimensions={1}, to_apply=%all_to_all.109.reduce_sub_computation | reduce | bytes 262148 | tf_op jit(solution)/shard_map/all_to_all | solution.py:100
  95.0 0.5 reshape.39
  95.5 0.2 copy.114
  95.7 0.7 copy.110
  (103 shorter events, 6.2 us)
Async XLA Ops:
  0.0 0.7 copy-start.2
  1.0 1.1 %copy-start.5 = (f32[128]{0:T(128)S(1)}, f32[128]{0:T(128)}, u32[]{:S(2)}) copy-start(f32[128]{0:T(128)} %param.13) | copy-start | bytes 1540
  1.0 1.1 %copy-start.6 = (s32[128]{0:T(128)S(1)}, s32[128]{0:T(128)}, u32[]{:S(2)}) copy-start(s32[128]{0:T(128)} %param.11) | copy-start | bytes 1540
  1.0 1.1 %copy-start.7 = (s32[128]{0:T(128)S(1)}, s32[128]{0:T(128)}, u32[]{:S(2)}) copy-start(s32[128]{0:T(128)} %param.12) | copy-start | bytes 1540
  1.0 1.4 %copy-start.1 = (s32[2,128,128]{2,1,0:T(8,128)S(1)}, s32[2,128,128]{2,1,0:T(8,128)}, u32[]{:S(2)}) copy-start(s32[2,128,128]{2,1,0:T(8,128)} %param.9) | copy-start | bytes 393220
  2.1 0.9 copy-start
  4.5 13.1 %all-to-all-start = ((f32[5,128,128]{2,0,1:T(8,128)}), f32[5,128,128]{2,0,1:T(8,128)S(1)}, u32[]{:S(2)}, u32[]{:S(2)}) async-start(f32[5,128,128]{2,0,1:T(8,128)} %pad_maximum_fusion), calls=%async_computation | async-start | bytes 1048576 | tf_op jit(solution)/shard_map/all_to_all | solution.py:96
  17.6 15.1 %all-to-all-start.3 = ((f32[3,128,128]{2,0,1:T(4,128)}), f32[3,128,128]{2,0,1:T(4,128)S(1)}, u32[]{:S(2)}, u32[]{:S(2)}) async-start(f32[3,128,128]{2,0,1:T(4,128)} %copy.98), calls=%async_computation.3 | async-start | bytes 524288 | tf_op jit(solution)/shard_map/all_to_all | solution.py:87
  24.5 0.7 copy-start.4
  32.7 7.9 %all-to-all-start.1 = ((f32[4,1,8192]{2,1,0:T(1,128)}), f32[4,1,8192]{2,1,0:T(1,128)S(1)}, u32[]{:S(2)}, u32[]{:S(2)}) async-start(f32[4,1,8192]{2,1,0:T(1,128)} %reshape.34), calls=%async_computation.1 | async-start | bytes 262144 | tf_op jit(solution)/shard_map/all_to_all | solution.py:100
  43.6 10.9 %all-to-all-start.2 = ((f32[2,128,128]{2,0,1:T(2,128)}), f32[2,128,128]{2,0,1:T(2,128)S(1)}, u32[]{:S(2)}, u32[]{:S(2)}) async-start(f32[2,128,128]{2,0,1:T(2,128)} %copy.94), calls=%async_computation.2 | async-start | bytes 262144 | tf_op jit(solution)/shard_map/all_to_all | solution.py:87
  54.6 0.7 copy-start.3
where the time goes:
time: 97 us; the launch traced here: 96.3 us
  waiting for transfers between devices  25.4 us (26%)
  blocking collectives  23.7 us (24%)
  local copies, waits for them, and re-layouts  18.9 us (19%)
  starting transfers between devices  17.6 us (18%)
  other arithmetic  9.41 us (10%)
  between operations  0.99 us (1%)
    all_to_all x2, waiting for transfers between devices, to_span(): lax.all_to_all(turned, 'span', split_axis=1, concat_axis=2, tiled=True)  13.2 us
    all_to_all x2, starting transfers between devices, to_span(): lax.all_to_all(turned, 'span', split_axis=1, concat_axis=2, tiled=True)  10 us
    all_to_all x1, blocking collectives, span_return(): lax.all_to_all(lines, 'span', split_axis=2, concat_axis=1, tiled=True)  9.74 us
    unnamed x26, local copies, waits for them, and re-layouts  9.18 us
    all_to_all x1, waiting for transfers between devices, to_chord(): lax.all_to_all(block, 'chord', split_axis=1, concat_axis=2, tiled=True)  7.84 us
    all_to_all x1, blocking collectives, to_chord(): lax.all_to_all(block, 'chord', split_axis=1, concat_axis=2, tiled=True)  6.99 us
    all_to_all x1, blocking collectives, from_chord(): lax.all_to_all(lines, 'chord', split_axis=2, concat_axis=1, tiled=True)  6.99 us
    all_to_all x1, waiting for transfers between devices, from_chord(): lax.all_to_all(lines, 'chord', split_axis=2, concat_axis=1, tiled=True)  4.36 us
  transfers between devices with their start and end apart: 4, of which 4 were waited for; matrix products, arithmetic and copies ran while one was open for 3% of the time, Pallas kernels for 0%

commit v1 on v0

--- a/solution.py
+++ b/solution.py
@@ -97,7 +97,10 @@
 
 
 def from_chord(lines):
-    return lax.all_to_all(lines, "chord", split_axis=2, concat_axis=1, tiled=True)
+    return jnp.concatenate(
+        lax.all_to_all(jnp.stack(jnp.split(lines, lax.axis_size("chord"), axis=2)), "chord", 0, 0),
+        axis=1,
+    )
 
 
 def per_device(pressure, fill_state, perm_class, perm_table, inlet_span, inlet_chord, inlet_rate):

time: 97 us -> 92.7 us (0.956)
  local copies, waits for them, and re-layouts: 18.9 us -> 15.3 us
  other arithmetic: 9.41 us -> 8 us
    unnamed x26 -> x22, local copies, waits for them, and re-layouts: 9.18 us -> 6.53 us
    all_to_all x2 -> x0, other arithmetic: 2.04 us -> none  [from_chord(): lax.all_to_all(lines, 'chord', split_axis=2, concat_axis=1, tiled=True)]
    all_to_all x5 -> x0, local copies, waits for them, and re-layouts: 1.65 us -> none  [from_chord(): lax.all_to_all(lines, 'chord', split_axis=2, concat_axis=1, tiled=True)]
where the time goes in v1:
time: 92.7 us; the launch traced here: 92.1 us
  waiting for transfers between devices  26.2 us (28%)
  blocking collectives  23.7 us (26%)
  starting transfers between devices  17.6 us (19%)
  local copies, waits for them, and re-layouts  15.3 us (17%)
  other arithmetic  8 us (9%)
  between operations  0.96 us (1%)
    all_to_all x2, waiting for transfers between devices, to_span(): lax.all_to_all(turned, 'span', split_axis=1, concat_axis=2, tiled=True)  14 us
    all_to_all x2, starting transfers between devices, to_span(): lax.all_to_all(turned, 'span', split_axis=1, concat_axis=2, tiled=True)  10 us
    all_to_all x1, blocking collectives, span_return(): lax.all_to_all(lines, 'span', split_axis=2, concat_axis=1, tiled=True)  9.74 us
    all_to_all x1, waiting for transfers between devices, to_chord(): lax.all_to_all(block, 'chord', split_axis=1, concat_axis=2, tiled=True)  7.85 us
    all_to_all x1, blocking collectives, from_chord(): lax.all_to_all(jnp.stack(jnp.split(lines, lax.axis_size('chord'), axis=2)...  6.99 us
    all_to_all x1, blocking collectives, to_chord(): lax.all_to_all(block, 'chord', split_axis=1, concat_axis=2, tiled=True)  6.99 us
    unnamed x22, local copies, waits for them, and re-layouts  6.53 us
    all_to_all x1, waiting for transfers between devices, from_chord(): lax.all_to_all(jnp.stack(jnp.split(lines, lax.axis_size('chord'), axis=2)...  4.36 us
  transfers between devices with their start and end apart: 4, of which 4 were waited for; matrix products, arithmetic and copies ran while one was open for 3% of the time, Pallas kernels for 0%

profile of v1, /device:TPU:0, one launch (start us, length us, event | category | flops | bytes accessed | tf_op | source)
XLA Modules:
  0.0 92.1 jit_solution(2383944226805564542)
XLA Ops:
  0.0 0.7 copy-done.2
  0.7 0.3 slice_reduce_fusion.7
  1.0 1.0 %copy.104 = f32[2,128,128]{2,0,1:T(2,128)S(1)} copy(f32[2,128,128]{2,1,0:T(8,128)} %param.7) | data formatting | bytes 262144 | tf_op args[0]
  2.1 0.2 fusion.16
  2.4 0.6 copy-done
  3.0 0.6 fusion.13
  3.5 1.0 %pad_maximum_fusion = f32[5,128,128]{2,0,1:T(8,128)} fusion(f32[2,128,128]{2,0,1:T(2,128)S(1)} %copy.104, f32[1,128,128]{2,0,1:T(1,128)S(1)} %bitcast.128, f32[2,128,128]{2,0,1:T(2,128)S(1)} %fusion.13), kind=kLoop, calls=%fused_computation | loop fusion | flops 163840 | bytes 655360 | tf_op jit(solution)/shard_map/concatenate | solution.py:130
  4.5 4.3 %all-to-all-start = ((f32[5,128,128]{2,0,1:T(8,128)}), f32[5,128,128]{2,0,1:T(8,128)S(1)}, u32[]{:S(2)}, u32[]{:S(2)}) async-start(f32[5,128,128]{2,0,1:T(8,128)} %pad_maximum_fusion), calls=%async_computation | async-start | bytes 1048576 | tf_op jit(solution)/shard_map/all_to_all | solution.py:96
  8.8 0.1 maximum_bitcast_fusion
  8.9 0.8 copy.114
  9.8 7.8 %all-to-all-done = f32[5,128,128]{2,0,1:T(8,128)S(1)} async-done(((f32[5,128,128]{2,0,1:T(8,128)}), f32[5,128,128]{2,0,1:T(8,128)S(1)}, u32[]{:S(2)}, u32[]{:S(2)}) %all-to-all-start) | async-done | bytes 327712 | tf_op jit(solution)/shard_map/all_to_all | solution.py:96
  17.6 6.5 %all-to-all-start.3 = ((f32[3,128,128]{2,0,1:T(4,128)}), f32[3,128,128]{2,0,1:T(4,128)S(1)}, u32[]{:S(2)}, u32[]{:S(2)}) async-start(f32[3,128,128]{2,0,1:T(4,128)} %copy.114), calls=%async_computation.3 | async-start | bytes 524288 | tf_op jit(solution)/shard_map/all_to_all | solution.py:87
  24.5 0.6 copy-done.4
  25.2 0.1 fusion.2
  25.3 0.7 pad_maximum_fusion.1
  26.0 6.7 %all-to-all-done.3 = f32[3,128,128]{2,0,1:T(4,128)S(1)} async-done(((f32[3,128,128]{2,0,1:T(4,128)}), f32[3,128,128]{2,0,1:T(4,128)S(1)}, u32[]{:S(2)}, u32[]{:S(2)}) %all-to-all-start.3) | async-done | bytes 196640 | tf_op jit(solution)/shard_map/all_to_all | solution.py:87
  32.7 3.3 %all-to-all-start.1 = ((f32[4,2,32,128]{3,2,1,0:T(8,128)}), f32[4,2,32,128]{3,2,1,0:T(8,128)S(1)}, u32[]{:S(2)}, u32[]{:S(2)}) async-start(f32[4,2,32,128]{3,2,1,0:T(8,128)} %pad_maximum_fusion.1), calls=%async_computation.1 | async-start | bytes 262144 | tf_op jit(solution)/shard_map/all_to_all | solution.py:101
  36.2 4.4 %all-to-all-done.1 = f32[4,2,32,128]{3,2,1,0:T(8,128)S(1)} async-done(((f32[4,2,32,128]{3,2,1,0:T(8,128)}), f32[4,2,32,128]{3,2,1,0:T(8,128)S(1)}, u32[]{:S(2)}, u32[]{:S(2)}) %all-to-all-start.1) | async-done | bytes 131104 | tf_op jit(solution)/shard_map/all_to_all | solution.py:101
  40.6 0.8 copy.110
  41.4 3.6 %all-to-all-start.2 = ((f32[2,128,128]{2,0,1:T(2,128)}), f32[2,128,128]{2,0,1:T(2,128)S(1)}, u32[]{:S(2)}, u32[]{:S(2)}) async-start(f32[2,128,128]{2,0,1:T(2,128)} %copy.110), calls=%async_computation.2 | async-start | bytes 262144 | tf_op jit(solution)/shard_map/all_to_all | solution.py:87
  45.0 7.3 %all-to-all-done.2 = f32[2,128,128]{2,0,1:T(2,128)S(1)} async-done(((f32[2,128,128]{2,0,1:T(2,128)}), f32[2,128,128]{2,0,1:T(2,128)S(1)}, u32[]{:S(2)}, u32[]{:S(2)}) %all-to-all-start.2) | async-done | bytes 131104 | tf_op jit(solution)/shard_map/all_to_all | solution.py:87
  52.3 0.7 copy-done.3
  53.0 0.1 negate_divide_fusion.2
  53.4 0.2 fusion.44
  53.6 0.1 fusion.60
  54.1 0.1 fusion.43
  54.2 0.1 fusion.58
  54.6 0.1 fusion.42
  54.8 0.1 fusion.56
  55.2 0.1 fusion.41
  55.3 0.1 fusion.54
  55.8 0.1 fusion.40
  55.9 0.1 fusion.52
  56.3 0.1 fusion.39
  56.5 0.1 fusion.50
  56.9 0.1 fusion.38
  57.1 0.1 fusion.48
  57.7 0.5 copy.118
  58.2 1.4 %reshape.50 = f32[8,1,4096]{2,1,0:T(1,128)S(1)} reshape(f32[1024,2,16]{2,1,0:T(2,128)S(1)} %bitcast.105) | data formatting | bytes 262144
  59.7 9.7 %all_to_all.94 = f32[8,1,4096]{2,1,0:T(1,128)S(1)} all-to-all(f32[8,1,4096]{2,1,0:T(1,128)S(1)} %reshape.50), channel_id=1, replica_groups=mesh['span'=8,'chord'=4] {'span'}, dimensions={0} | all-to-all | bytes 262144 | tf_op jit(solution)/shard_map/all_to_all | solution.py:91
  69.4 0.5 broadcast.342
  69.9 1.0 %reduce.16 = f32[8,4096]{1,0:T(8,128)S(1)} reduce(f32[8,1,4096]{2,1,0:T(1,128)S(1)} %all_to_all.94, f32[]{:T(128)} %broadcast.342), dimensions={1}, to_apply=%all_to_all.78.reduce_sub_computation | reduce | bytes 262148 | tf_op jit(solution)/shard_map/all_to_all | solution.py:91
  70.9 1.4 %reshape.51 = f32[1024,2,16]{2,1,0:T(2,128)S(1)} reshape(f32[8,4096]{1,0:T(8,128)S(1)} %reduce.16) | data formatting | bytes 262144
  72.3 0.4 copy.126
  72.7 0.1 copy.121
  72.8 7.0 %all_to_all.95 = f32[2,128,128]{2,0,1:T(2,128)S(1)} all-to-all(f32[2,128,128]{2,0,1:T(2,128)S(1)} %copy.121), channel_id=1, replica_groups=mesh['span'=8,'chord'=4] {'chord'}, dimensions={1} | all-to-all | bytes 262144 | tf_op jit(solution)/shard_map/all_to_all | solution.py:96
  79.8 0.1 negate_divide_fusion
  80.3 0.2 fusion.34
  80.5 0.1 fusion.74
  80.9 0.1 fusion.33
  81.1 0.1 fusion.72
  81.5 0.1 fusion.32
  81.7 0.1 fusion.70
  82.1 0.1 fusion.31
  82.2 0.1 fusion.68
  82.6 0.1 fusion.30
  82.8 0.1 fusion.66
  83.2 0.1 fusion.29
  83.4 0.1 fusion.64
  83.8 0.1 fusion.28
  83.9 0.1 fusion.62
  84.1 0.1 fusion.27
  84.4 7.0 %all_to_all.96 = f32[4,2,32,128]{3,2,1,0:T(8,128)S(1)} all-to-all(f32[4,2,32,128]{3,2,1,0:T(8,128)S(1)} %pad_maximum_fusion.2), channel_id=1, replica_groups=mesh['span'=8,'chord'=4] {'chord'}, dimensions={0} | all-to-all | bytes 262144 | tf_op jit(solution)/shard_map/all_to_all | solution.py:101
  91.4 0.7 copy.124
  (97 shorter events, 5.2 us)
Async XLA Ops:
  0.0 0.7 copy-start.2
  1.0 1.1 %copy-start.5 = (f32[128]{0:T(128)S(1)}, f32[128]{0:T(128)}, u32[]{:S(2)}) copy-start(f32[128]{0:T(128)} %param.13) | copy-start | bytes 1540
  1.0 1.1 %copy-start.6 = (s32[128]{0:T(128)S(1)}, s32[128]{0:T(128)}, u32[]{:S(2)}) copy-start(s32[128]{0:T(128)} %param.11) | copy-start | bytes 1540
  1.0 1.1 %copy-start.7 = (s32[128]{0:T(128)S(1)}, s32[128]{0:T(128)}, u32[]{:S(2)}) copy-start(s32[128]{0:T(128)} %param.12) | copy-start | bytes 1540
  1.0 1.4 %copy-start.1 = (s32[2,128,128]{2,1,0:T(8,128)S(1)}, s32[2,128,128]{2,1,0:T(8,128)}, u32[]{:S(2)}) copy-start(s32[2,128,128]{2,1,0:T(8,128)} %param.9) | copy-start | bytes 393220
  2.1 0.9 copy-start
  4.5 13.1 %all-to-all-start = ((f32[5,128,128]{2,0,1:T(8,128)}), f32[5,128,128]{2,0,1:T(8,128)S(1)}, u32[]{:S(2)}, u32[]{:S(2)}) async-start(f32[5,128,128]{2,0,1:T(8,128)} %pad_maximum_fusion), calls=%async_computation | async-start | bytes 1048576 | tf_op jit(solution)/shard_map/all_to_all | solution.py:96
  17.6 15.1 %all-to-all-start.3 = ((f32[3,128,128]{2,0,1:T(4,128)}), f32[3,128,128]{2,0,1:T(4,128)S(1)}, u32[]{:S(2)}, u32[]{:S(2)}) async-start(f32[3,128,128]{2,0,1:T(4,128)} %copy.114), calls=%async_computation.3 | async-start | bytes 524288 | tf_op jit(solution)/shard_map/all_to_all | solution.py:87
  24.5 0.7 copy-start.4
  32.7 7.9 %all-to-all-start.1 = ((f32[4,2,32,128]{3,2,1,0:T(8,128)}), f32[4,2,32,128]{3,2,1,0:T(8,128)S(1)}, u32[]{:S(2)}, u32[]{:S(2)}) async-start(f32[4,2,32,128]{3,2,1,0:T(8,128)} %pad_maximum_fusion.1), calls=%async_computation.1 | async-start | bytes 262144 | tf_op jit(solution)/shard_map/all_to_all | solution.py:101
  41.4 10.9 %all-to-all-start.2 = ((f32[2,128,128]{2,0,1:T(2,128)}), f32[2,128,128]{2,0,1:T(2,128)S(1)}, u32[]{:S(2)}, u32[]{:S(2)}) async-start(f32[2,128,128]{2,0,1:T(2,128)} %copy.110), calls=%async_computation.2 | async-start | bytes 262144 | tf_op jit(solution)/shard_map/all_to_all | solution.py:87
  52.3 0.7 copy-start.3
